TPU v7x, 32 devices: a whole 2x2x4 slice. The times are simulated.
32 devices in a mesh: row: 4 (over y, core), col: 8 (over z, x).
Axes of the slice: x: 2, y: 2, z: 4, core: 2. Of those that a mesh axis runs over, the one named last changes fastest.
Arguments:
- front: float32 [12288, 12288], P('row', 'col'), may hold values from -6 to 6
- delayed: float32 [64, 12288], P('col', 'row'), may hold values from -6 to 6
- dest: int32 [64], P('col'), may hold values from 0 to 1023, as said below
- pivots: int32 [1024], replicated, may hold values from 0 to 12287, as said below
- pair_flags: int32 [1024], replicated, may hold values from 0 to 1, as said below
- linv: float32 [4, 256, 256], replicated, as said below
- dinv_diag: float32 [1024], replicated, may hold values from -0.1 to 0.1
- dinv_off: float32 [1024], replicated, may hold values from -0.08 to 0.08
Outputs:
- trailing: float32 [12288, 12288], P('row', 'col')
- factor: float32 [12288, 1024], P('row')
Inputs may be any that keep to these rules, and one draw needn't show every extreme that they name: Distinct front columns; slots p * 256 to (p + 1) * 256 - 1 are panel p's pivots. Each block of 1536 columns held by one index of col contains exactly 128 of them. `pair_flags`: A 1 at slot s joins slots s and s + 1 into one 2x2 block; no two 1s are adjacent and the last slot of a panel holds 0. `dest`: several delayed columns may share a slot. Of the 8 delayed columns held by one index of col, at most 2 go to pivot columns held by the same index of col. `linv`: each panel's matrix is unit lower triangular: ones on the diagonal, zeros above it.
All inputs are finite; a program needn't handle non-finite values.
Results may differ from a plain program's by a relative error of at most 0.00015.
Values sent between devices are 32-bit elements; how exact they have to be, the bound alone decides.
A program may use at most 192 MiB of HBM per device.

v0:
```python
import jax
import jax.numpy as jnp
from jax import lax
from jax.sharding import PartitionSpec as P

CAP = 2
precise = lax.Precision.HIGHEST


def broadcast(block, axis, holder):
    block = jnp.where(lax.axis_index(axis) == holder, block, jnp.zeros_like(block))
    return lax.psum(block, axis)


def pair_scale(scaled, pair_bits, diag_part, off_part):
    coupled = pair_bits.astype(jnp.float32) * off_part
    zero_col = jnp.zeros_like(scaled[:, :1])
    shifted_next = jnp.concatenate([scaled[:, 1:], zero_col], axis=1)
    shifted_prev = jnp.concatenate([zero_col, scaled[:, :-1]], axis=1)
    coupled_prev = jnp.concatenate([jnp.zeros_like(coupled[:1]), coupled[:-1]])
    return scaled * diag_part + shifted_next * coupled + shifted_prev * coupled_prev


def select_columns(matrix, wanted, anchor):
    block_width = matrix.shape[1]
    relative = wanted - anchor
    inside = (relative >= 0) & (relative < block_width)
    clipped = jnp.clip(relative, 0, block_width - 1)
    return jnp.where(inside[None, :], jnp.take(matrix, clipped, axis=1), 0.0)


def select_rows(matrix, wanted, anchor):
    block_height = matrix.shape[0]
    relative = wanted - anchor
    inside = (relative >= 0) & (relative < block_height)
    clipped = jnp.clip(relative, 0, block_height - 1)
    return jnp.where(inside[:, None], jnp.take(matrix, clipped, axis=0), 0.0)


def body(front, delayed, dest, pivots, pair_flags, linv, dinv_diag, dinv_off):
    col_count = lax.axis_size("col")
    rows_blk, cols_blk = front.shape
    row_start = lax.axis_index("row") * rows_blk
    col_start = lax.axis_index("col") * cols_blk
    panel_count = linv.shape[0]
    panel_width = linv.shape[1]
    slot_total = pivots.shape[0]
    slot_ids = jnp.arange(slot_total, dtype=jnp.int32)
    owner_ids = jnp.arange(col_count, dtype=jnp.int32)
    slot_hit = dest[:, None] == slot_ids[None, :]
    targets = jnp.sum(jnp.where(slot_hit, pivots[None, :], 0), axis=1)
    owners = targets // cols_blk
    within = targets - owners * cols_blk
    owner_hit = (owners[:, None] == owner_ids[None, :]).astype(jnp.int32)
    earlier = jnp.cumsum(owner_hit, axis=0) - owner_hit
    rank_in = jnp.sum(earlier * owner_hit, axis=1)
    slot_pos = jnp.arange(CAP, dtype=jnp.int32)
    placed = (owner_hit[:, :, None] > 0) & (rank_in[:, None, None] == slot_pos[None, None, :])
    send_vals = jnp.einsum("kos,kr->osr", placed.astype(jnp.float32), delayed, precision=precise)
    send_cols = jnp.sum(jnp.where(placed, within[:, None, None] + 1, 0), axis=0) - 1
    recv_vals, recv_cols = (
        lax.all_to_all(send_vals, "col", split_axis=0, concat_axis=0, tiled=True),
        lax.all_to_all(send_cols, "col", split_axis=0, concat_axis=0, tiled=True),
    )
    flat_vals = recv_vals.reshape(-1, rows_blk)
    flat_cols = recv_cols.reshape(-1)
    col_ids = jnp.arange(cols_blk, dtype=jnp.int32)
    col_hit = (flat_cols[:, None] == col_ids[None, :]).astype(jnp.float32)
    current = front + lax.dot_general(
        flat_vals, col_hit, (((0,), (0,)), ((), ())), precision=precise
    )
    factors = []
    piv_owner = pivots // cols_blk
    piv_hit = (piv_owner[:, None] == owner_ids[None, :]).astype(jnp.int32)
    piv_rank = jnp.sum((jnp.cumsum(piv_hit, axis=0) - piv_hit) * piv_hit, axis=1)
    per_owner = slot_total // col_count
    owned_here = piv_owner == lax.axis_index("col")
    rank_ids = jnp.arange(per_owner, dtype=jnp.int32)
    own_slots = jnp.sum(
        jnp.where(
            owned_here[None, :] & (piv_rank[None, :] == rank_ids[:, None]), slot_ids[None, :], 0
        ),
        axis=1,
    )
    compact = select_columns(current, pivots[own_slots], col_start)
    gathered = lax.all_gather(compact, "col", axis=1, tiled=True)
    every_panel = jnp.take(gathered, piv_owner * per_owner + piv_rank, axis=1)
    previous = []
    for panel_index in range(panel_count):
        offset = panel_index * panel_width
        panel_cols = every_panel[:, offset : offset + panel_width]
        for cols_before, rows_before in previous:
            panel_cols = panel_cols - lax.dot_general(
                cols_before,
                rows_before[offset : offset + panel_width],
                (((1,), (1,)), ((), ())),
                precision=precise,
            )
        finish_offset = panel_index * panel_width
        finish_scaled = jnp.dot(panel_cols, jnp.transpose(linv[panel_index]), precision=precise)
        finish_columns = pair_scale(
            finish_scaled,
            pair_flags[finish_offset : finish_offset + panel_width],
            dinv_diag[finish_offset : finish_offset + panel_width],
            dinv_off[finish_offset : finish_offset + panel_width],
        )
        root_row = col_start // rows_blk
        slice_start = jnp.clip(col_start - row_start, 0, rows_blk - cols_blk)
        root_piece = lax.dynamic_slice_in_dim(finish_scaled, slice_start, cols_blk, 0)
        col_scaled = broadcast(root_piece, "row", root_row)
        current = current - lax.dot_general(
            finish_columns, col_scaled, (((1,), (1,)), ((), ())), precision=precise
        )
        factors.append(finish_columns)
        if panel_index + 1 < panel_count:
            pivot_part = select_rows(finish_scaled, pivots, row_start)
            pivot_rows = lax.psum(pivot_part, "row")
            previous.append((finish_columns, pivot_rows))
    row_ids = row_start + jnp.arange(rows_blk, dtype=jnp.int32)
    row_in = jnp.any(row_ids[:, None] == pivots[None, :], axis=1)
    col_in = jnp.any((col_start + col_ids)[:, None] == pivots[None, :], axis=1)
    trailing = jnp.where(row_in[:, None] | col_in[None, :], 0.0, current)
    factor = jnp.concatenate(factors, axis=1)
    return (trailing, factor)


def solution(mesh):
    return jax.shard_map(
        body,
        mesh=mesh,
        in_specs=(P("row", "col"), P("col", "row"), P("col"), P(), P(), P(), P(), P()),
        out_specs=(P("row", "col"), P("row", None)),
        check_vma=False,
    )
```

profile of v0, /device:TPU:0, one launch (start us, length us, event | category | flops | bytes accessed | tf_op | source)
XLA Modules:
  0.0 721.7 jit_solution(9475887452106300543)
XLA Ops:
  9.2 7.3 %all-to-all-start.1 = ((s32[8,1,2]{2,1,0:T(1,128)}), s32[8,1,2]{2,1,0:T(1,128)S(1)}, u32[]{:S(2)}, u32[]{:S(2)}) async-start(s32[8,1,2]{2,1,0:T(1,128)} %copy.32), calls=%async_computation.1 | async-start | bytes 8192 | tf_op jit(solution)/shard_map/all_to_all | solution.py:63
  18.2 2.3 reduce-window.6
  22.9 6.0 all-to-all-start
  30.2 6.4 all-to-all-done
  36.8 18.0 %convolution_add_fusion = f32[3072,1536]{1,0:T(8,128)} fusion(f32[3072,1536]{1,0:T(8,128)} %param.10, f32[16,3072]{1,0:T(8,128)S(1)} %reshape.189, s32[16]{0:T(128)S(1)} %eq.152), kind=kOutput, calls=%fused_computation.7 | convolution fusion | flops 910712832 | bytes 37945408 | tf_op jit(solution)/shard_map/dot_general | solution.py:69
  54.8 18.7 %copy.33 = f32[3072,1536]{0,1:T(8,128)} copy(f32[3072,1536]{1,0:T(8,128)} %convolution_add_fusion) | data formatting | bytes 37748736 | tf_op jit(solution)/shard_map/add | solution.py:69
  73.4 8.2 %gather_fusion.1 = f32[128,3072]{1,0:T(8,128)S(1)} fusion(f32[3072,1536]{0,1:T(8,128)} %copy.33, s32[1024]{0:T(1024)S(1)} %pad_clamp_fusion), kind=kCustom, calls=%fused_computation.4 | custom fusion | bytes 3146240 | tf_op jit(solution)/shard_map/jit(_take)/gather | solution.py:29
  84.1 173.5 %all-gather.2.cloned.1.call-done = f32[3072,1024]{0,1:T(8,128)} async-done(((f32[3072,128]{0,1:T(8,128)}), f32[3072,1024]{0,1:T(8,128)}) %all-gather.2.cloned.1.call-update) | async-done | bytes 12582928 | tf_op jit(solution)/shard_map/all_gather | solution.py:86
  257.6 16.5 %gather_fusion.2 = f32[1024,3072]{1,0:T(8,128)} fusion(f32[3072,1024]{0,1:T(8,128)} %all-gather.2.cloned.1.call-done, s32[1024]{0:T(1024)S(1)} %broadcast_clamp_fusion), kind=kCustom, calls=%fused_computation.5 | custom fusion | bytes 25169920 | tf_op jit(solution)/shard_map/jit(_take)/gather | solution.py:87
  274.1 12.6 %copy.34 = f32[1024,3072]{0,1:T(8,128)} copy(f32[1024,3072]{1,0:T(8,128)} %gather_fusion.2) | data formatting | bytes 25165824 | tf_op jit(solution)/shard_map/jit(_take)/gather | solution.py:87
  286.7 12.4 %select_bitcast_fusion = f32[3072,1024]{1,0:T(8,128)} fusion(f32[1024,3072]{0,1:T(8,128)} %copy.34, pred[1024]{0:T(1024)(128)(4,1)S(1)} %compare_and_fusion.2), kind=kLoop, calls=%fused_computation.9 | loop fusion | flops 3145728 | bytes 25166848 | tf_op jit(solution)/shard_map/jit(_take)/select_n | solution.py:87
  299.1 4.8 fusion
  304.0 3.7 fusion.40
  307.7 2.3 copy.35
  310.0 5.3 gather_fusion.3
  316.9 5.3 multiply_add_fusion.3
  324.0 27.4 %all-reduce.14.cloned.1.call-done = f32[1024,256]{1,0:T(8,128)} async-done(((f32[1024,256]{1,0:T(8,128)}), f32[1024,256]{1,0:T(8,128)}) %all-reduce.14.cloned.1.call-update) | async-done | bytes 1048592 | tf_op jit(solution)/shard_map/psum | solution.py:117
  351.4 7.3 %convolution_subtract_fusion.5 = f32[3072,256]{1,0:T(8,128)S(1)} fusion(f32[3072,256]{0,1:T(8,128)S(1)} %multiply_add_fusion.3, f32[3072,1024]{1,0:T(8,128)} %select_bitcast_fusion, f32[1024,256]{1,0:T(8,128)} %all-reduce.14.cloned.1.call-done), kind=kOutput, calls=%fused_computation.17 | convolution fusion | flops 2416705536 | bytes 9699328 | tf_op jit(solution)/shard_map/dot_general | solution.py:93
  358.7 4.1 fusion.13
  364.4 3.3 fusion.39
  367.8 3.5 copy.36
  371.3 6.6 gather_fusion.4
  377.8 2.5 select_select_fusion.1
  380.7 7.0 multiply_add_fusion.2
  387.6 8.0 %convolution_subtract_fusion.4 = f32[3072,256]{1,0:T(8,128)} fusion(f32[3072,256]{0,1:T(8,128)S(1)} %multiply_add_fusion.3, f32[3072,1024]{1,0:T(8,128)} %select_bitcast_fusion, f32[1024,256]{1,0:T(8,128)S(1)} %copy-done.19), kind=kOutput, calls=%fused_computation.16 | convolution fusion | flops 2416705536 | bytes 9699328 | tf_op jit(solution)/shard_map/dot_general | solution.py:93
  397.3 8.3 %convolution_subtract_fusion.2 = f32[3072,256]{1,0:T(8,128)} fusion(f32[3072,256]{0,1:T(8,128)S(1)} %multiply_add_fusion.3, f32[3072,1024]{1,0:T(8,128)} %select_bitcast_fusion, f32[1024,256]{1,0:T(8,128)S(1)} %copy-done.19), kind=kOutput, calls=%fused_computation.14 | convolution fusion | flops 2416705536 | bytes 9699328 | tf_op jit(solution)/shard_map/dot_general | solution.py:93
  405.5 11.8 %all-reduce.16.cloned.1.call-done = f32[1024,256]{1,0:T(8,128)} async-done(((f32[1024,256]{1,0:T(8,128)}), f32[1024,256]{1,0:T(8,128)}) %all-reduce.16.cloned.1.call-update) | async-done | bytes 1048592 | tf_op jit(solution)/shard_map/psum | solution.py:117
  417.3 8.3 %convolution_subtract_fusion.3 = f32[3072,256]{1,0:T(8,128)S(1)} fusion(f32[3072,256]{1,0:T(8,128)} %convolution_subtract_fusion.4, f32[3072,256]{0,1:T(8,128)} %multiply_add_fusion.2, f32[1024,256]{1,0:T(8,128)} %all-reduce.16.cloned.1.call-done), kind=kOutput, calls=%fused_computation.15 | convolution fusion | flops 2416705536 | bytes 9699328 | tf_op jit(solution)/shard_map/dot_general | solution.py:93
  425.7 4.1 fusion.11
  429.8 1.7 copy-done.2
  431.4 3.3 fusion.38
  434.7 3.5 copy.37
  438.2 6.6 gather_fusion.5
  444.8 2.6 select_select_fusion
  447.7 7.0 multiply_add_fusion.1
  457.2 8.1 %convolution_subtract_fusion.1 = f32[3072,256]{1,0:T(8,128)} fusion(f32[3072,256]{1,0:T(8,128)S(1)} %copy-done.16, f32[3072,256]{0,1:T(8,128)S(1)} %copy-done.8, f32[1024,256]{1,0:T(8,128)} %all-reduce.16.cloned.1.call-done), kind=kOutput, calls=%fused_computation.13 | convolution fusion | flops 2416705536 | bytes 9699328 | tf_op jit(solution)/shard_map/dot_general | solution.py:93
  465.3 19.0 %all-reduce.18.cloned.1.call-done = f32[1024,256]{1,0:T(8,128)} async-done(((f32[1024,256]{1,0:T(8,128)}), f32[1024,256]{1,0:T(8,128)}) %all-reduce.18.cloned.1.call-update) | async-done | bytes 1048592 | tf_op jit(solution)/shard_map/psum | solution.py:117
  484.4 8.3 %convolution_subtract_fusion = f32[3072,256]{1,0:T(8,128)S(1)} fusion(f32[3072,256]{1,0:T(8,128)} %convolution_subtract_fusion.1, f32[3072,256]{0,1:T(8,128)} %multiply_add_fusion.1, f32[1024,256]{1,0:T(8,128)} %all-reduce.18.cloned.1.call-done), kind=kOutput, calls=%fused_computation.12 | convolution fusion | flops 2416705536 | bytes 9699328 | tf_op jit(solution)/shard_map/dot_general | solution.py:93
  492.7 4.3 fusion.9
  501.4 2.0 compare_reduce_fusion
  503.4 3.9 fusion.37
  512.0 5.4 pad_maximum_fusion
  517.4 12.6 %copy.38 = f32[3072,1024]{1,0:T(8,128)} copy(f32[3072,1024]{0,1:T(8,128)} %pad_maximum_fusion) | data formatting | bytes 25165824
  530.0 90.6 %all-reduce.20.cloned.1.call-done = (f32[1536,256]{0,1:T(8,128)}, f32[1536,256]{0,1:T(8,128)}, f32[1536,256]{0,1:T(8,128)}, f32[1536,256]{0,1:T(8,128)}) async-done(((f32[1536,256]{0,1:T(8,128)}, f32[1536,256]{0,1:T(8,128)}, f32[1536,256]{0,1:T(8,128)}, f32[1536,256]{0,1:T(8,128)}), (f32[1536,256]{0,1:T(8,128)}, f32[1536,256]{0,1:T(8,128)}, f32[1536,256]{0,1:T(8,128)}, ...) | async-done | bytes 6291472 | tf_op jit(solution)/shard_map/psum | solution.py:12
  620.6 19.9 %fusion.44 = f32[3072,1536]{1,0:T(8,128)} fusion(f32[3072,256]{0,1:T(8,128)} %multiply_add_fusion.1, f32[1536,256]{0,1:T(8,128)} %get-tuple-element.11), kind=kOutput, calls=%fused_computation.119 | convolution fusion | flops 14495514624 | bytes 23592960 | tf_op jit(solution)/shard_map/dot_general | solution.py:111
  640.5 18.5 %fusion.43 = f32[3072,1536]{1,0:T(8,128)} fusion(f32[3072,256]{0,1:T(8,128)S(1)} %copy-done.10, f32[1536,256]{0,1:T(8,128)S(1)} %copy-done.18), kind=kOutput, calls=%fused_computation.118 | convolution fusion | flops 14495514624 | bytes 23592960 | tf_op jit(solution)/shard_map/dot_general | solution.py:111
  659.0 17.9 %fusion.42 = f32[3072,1536]{1,0:T(8,128)} fusion(f32[3072,256]{0,1:T(8,128)S(1)} %multiply_add_fusion.3, f32[1536,256]{0,1:T(8,128)S(1)} %copy-done.17), kind=kOutput, calls=%fused_computation.117 | convolution fusion | flops 14495514624 | bytes 23592960 | tf_op jit(solution)/shard_map/dot_general | solution.py:111
  676.9 38.1 %subtract_select_fusion = f32[3072,1536]{1,0:T(8,128)} fusion(f32[3072,1536]{1,0:T(8,128)} %fusion.44, f32[3072,1536]{1,0:T(8,128)} %fusion.43, f32[3072,1536]{1,0:T(8,128)} %convolution_add_fusion, f32[3072,1536]{1,0:T(8,128)} %fusion.42, f32[3072,256]{0,1:T(8,128)} %copy-done.15, f32[1536,256]{0,1:T(8,128)} %get-tuple-element.14, ...), kind=kOutput, calls=%fused_computation.6 | convolution fusion | flops 14523826176 | bytes 99095040 | tf_op jit(solution)/shard_map/dot_general | solution.py:111
  (102 shorter events, 28.4 us)
Async XLA Ops:
  7.2 9.3 %copy-start = (f32[8,3072]{1,0:T(8,128)S(1)}, f32[8,3072]{1,0:T(8,128)}, u32[]{:S(2)}) copy-start(f32[8,3072]{1,0:T(8,128)} %param.11) | copy-start | bytes 294916
  9.2 13.7 %all-to-all-start.1 = ((s32[8,1,2]{2,1,0:T(1,128)}), s32[8,1,2]{2,1,0:T(1,128)S(1)}, u32[]{:S(2)}, u32[]{:S(2)}) async-start(s32[8,1,2]{2,1,0:T(1,128)} %copy.32), calls=%async_computation.1 | async-start | bytes 8192 | tf_op jit(solution)/shard_map/all_to_all | solution.py:63
  22.9 13.8 %all-to-all-start = ((f32[8,2,3072]{2,1,0:T(2,128)}), f32[8,2,3072]{2,1,0:T(2,128)S(1)}, u32[]{:S(2)}, u32[]{:S(2)}) async-start(f32[8,2,3072]{2,1,0:T(2,128)} %copy.31), calls=%async_computation | async-start | bytes 393216 | tf_op jit(solution)/shard_map/all_to_all | solution.py:62
  28.9 228.7 %all-gather.2.cloned.1.call-start = ((), (), s32[]{:S(2)}) async-start(), calls=%async_computation.2 | async-start | bytes 14155776 | tf_op jit(solution)/shard_map/all_gather | solution.py:86
  81.7 2.1 copy-start.20
  81.7 2.1 copy-start.21
  81.7 2.3 copy-start.11
  81.7 2.3 copy-start.22
  83.2 268.2 %all-reduce.14.cloned.1.call-start = ((), (), s32[]{:S(2)}) async-start(), calls=%async_computation.3 | async-start | bytes 2097152 | tf_op jit(solution)/shard_map/psum | solution.py:117
  304.0 3.7 copy-start.6
  316.7 100.6 %all-reduce.16.cloned.1.call-start = ((), (), s32[]{:S(2)}) async-start(), calls=%async_computation.4 | async-start | bytes 2097152 | tf_op jit(solution)/shard_map/psum | solution.py:117
  316.9 5.4 copy-start.7
  362.8 1.7 copy-start.4
  380.4 103.9 %all-reduce.18.cloned.1.call-start = ((), (), s32[]{:S(2)}) async-start(), calls=%async_computation.5 | async-start | bytes 2097152 | tf_op jit(solution)/shard_map/psum | solution.py:117
  380.7 7.0 copy-start.19
  387.6 8.0 %copy-start.5 = (f32[3072,256]{0,1:T(8,128)S(1)}, f32[3072,256]{0,1:T(8,128)}, u32[]{:S(2)}) copy-start(f32[3072,256]{0,1:T(8,128)} %copy-done.4) | copy-start | bytes 9437188
  429.7 1.7 copy-start.2
  447.5 173.2 %all-reduce.20.cloned.1.call-start = ((), (), s32[]{:S(2)}) async-start(), calls=%async_computation.6 | async-start | bytes 12582912 | tf_op jit(solution)/shard_map/psum | solution.py:12
  447.7 7.1 copy-start.3
  447.7 8.7 %copy-start.16 = (f32[3072,256]{1,0:T(8,128)S(1)}, f32[3072,256]{1,0:T(8,128)}, u32[]{:S(2)}) copy-start(f32[3072,256]{1,0:T(8,128)} %convolution_subtract_fusion.2) | copy-start | bytes 9437188
  454.7 2.5 copy-start.8
  497.0 1.7 copy-start.12
  503.4 4.6 copy-start.13
  508.0 3.0 copy-start.9
  508.0 4.0 copy-start.14
  509.3 1.7 copy-start.15
  620.6 19.9 %copy-start.10 = (f32[3072,256]{0,1:T(8,128)S(1)}, f32[3072,256]{0,1:T(8,128)}, u32[]{:S(2)}) copy-start(f32[3072,256]{0,1:T(8,128)} %multiply_add_fusion.2) | copy-start | bytes 9437188
  620.6 19.9 %copy-start.18 = (f32[1536,256]{0,1:T(8,128)S(1)}, f32[1536,256]{0,1:T(8,128)}, u32[]{:S(2)}) copy-start(f32[1536,256]{0,1:T(8,128)} %get-tuple-element.12) | copy-start | bytes 4718596
  640.5 18.5 %copy-start.17 = (f32[1536,256]{0,1:T(8,128)S(1)}, f32[1536,256]{0,1:T(8,128)}, u32[]{:S(2)}) copy-start(f32[1536,256]{0,1:T(8,128)} %get-tuple-element.13) | copy-start | bytes 4718596
  676.9 38.1 %copy-start.1 = (f32[8,3072]{1,0:T(8,128)S(1)}, f32[8,3072]{1,0:T(8,128)}, u32[]{:S(2)}) copy-start(f32[8,3072]{1,0:T(8,128)} %param.11) | copy-start | bytes 294916
Sparse Core Ops, SparseCore 0:
  83.3 174.2 all-gather.1
  316.8 34.4 all-reduce.13
  380.5 36.7 all-reduce.15
  447.6 36.7 all-reduce.17
  500.5 120.0 all-reduce.19
where the time goes:
time: 728 us; the launch traced here: 722 us
  waiting for transfers between devices  329 us (45%)
  matrix products  178 us (24%)
  local copies, waits for them, and re-layouts  124 us (17%)
  other arithmetic  61.7 us (8%)
  starting transfers between devices  14.6 us (2%)
  between operations  14.4 us (2%)
    all_gather x1, waiting for transfers between devices, body(): gathered = lax.all_gather(compact, 'col', axis=1, tiled=True)  174 us
    dot_general x4, matrix products, body(): lax.dot_general(finish_columns, col_scaled, (((1,), (1,)), ((), ())), pre...  94.3 us
    psum x1, waiting for transfers between devices, broadcast(): return lax.psum(block, axis)  90.6 us
    psum x3, waiting for transfers between devices, body(): pivot_rows = lax.psum(pivot_part, 'row')  58.2 us
    dot_general x6, matrix products, body(): lax.dot_general(cols_before, rows_before[offset:offset + panel_width], ((...  48.4 us
    gather x2, local copies, waits for them, and re-layouts, body(): every_panel = jnp.take(gathered, piv_owner * per_owner + piv_rank, axis=1)  29.1 us
    unnamed x47, local copies, waits for them, and re-layouts  21.9 us
    add x4, other arithmetic, pair_scale(): scaled * diag_part + shifted_next * coupled + shifted_prev * coupled_prev  20.7 us
  transfers between devices with their start and end apart: 7, of which 6 were waited for; matrix products, arithmetic and copies ran while one was open for 11% of the time, Pallas kernels for 0%

commit v1 on v0

--- a/solution.py
+++ b/solution.py
@@ -83,7 +83,10 @@
         axis=1,
     )
     compact = select_columns(current, pivots[own_slots], col_start)
-    gathered = lax.all_gather(compact, "col", axis=1, tiled=True)
+    _put_ranges = lambda z_in: jnp.concatenate(
+        jax.lax.all_to_all(jnp.stack(jax.lax.axis_size("col") * [z_in], 0), "col", 0, 0), 1
+    )
+    gathered = _put_ranges(compact)
     every_panel = jnp.take(gathered, piv_owner * per_owner + piv_rank, axis=1)
     previous = []
     for panel_index in range(panel_count):

time: 728 us -> 837 us (1.15)
  waiting for transfers between devices: 329 us -> 427 us
    all_to_all x0 -> x1, waiting for transfers between devices: none -> 270 us  [body(): jax.lax.all_to_all(jnp.stack(jax.lax.axis_size('col') * [z_in], 0), 'col'...]
    all_gather x1 -> x0, waiting for transfers between devices: 174 us -> none  [body(): gathered = lax.all_gather(compact, 'col', axis=1, tiled=True)]
  transfers between devices with their start and end apart: 7 -> 7, of which waited for: 6 -> 6; matrix products, arithmetic and copies ran while one was open for 11% -> 10% of each run, Pallas kernels for 0% -> 0%
where the time goes in v1:
time: 837 us; the launch traced here: 830 us
  waiting for transfers between devices  427 us (51%)
  matrix products  178 us (21%)
  local copies, waits for them, and re-layouts  130 us (16%)
  other arithmetic  60.1 us (7%)
  starting transfers between devices  20 us (2%)
  between operations  14.4 us (2%)
    all_to_all x1, waiting for transfers between devices, body(): jax.lax.all_to_all(jnp.stack(jax.lax.axis_size('col') * [z_in], 0), 'col'...  270 us
    dot_general x4, matrix products, body(): lax.dot_general(finish_columns, col_scaled, (((1,), (1,)), ((), ())), pre...  94.3 us
    psum x1, waiting for transfers between devices, broadcast(): return lax.psum(block, axis)  90.9 us
    psum x3, waiting for transfers between devices, body(): pivot_rows = lax.psum(pivot_part, 'row')  59.2 us
    dot_general x6, matrix products, body(): lax.dot_general(cols_before, rows_before[offset:offset + panel_width], ((...  48.3 us
    gather x2, local copies, waits for them, and re-layouts, body(): every_panel = jnp.take(gathered, piv_owner * per_owner + piv_rank, axis=1)  29.1 us
    unnamed x47, local copies, waits for them, and re-layouts  21.9 us
    add x4, other arithmetic, pair_scale(): scaled * diag_part + shifted_next * coupled + shifted_prev * coupled_prev  20.5 us
  transfers between devices with their start and end apart: 7, of which 6 were waited for; matrix products, arithmetic and copies ran while one was open for 10% of the time, Pallas kernels for 0%

profile of v1, /device:TPU:0, one launch (start us, length us, event | category | flops | bytes accessed | tf_op | source)
XLA Modules:
  0.0 829.8 jit_solution(12624039342449714555)
XLA Ops:
  9.2 7.3 all-to-all-start.1
  18.2 2.3 reduce-window.6
  22.9 6.0 all-to-all-start
  30.2 6.5 all-to-all-done
  36.8 18.0 %convolution_add_fusion = f32[3072,1536]{1,0:T(8,128)} fusion(f32[3072,1536]{1,0:T(8,128)} %param.10, f32[16,3072]{1,0:T(8,128)S(1)} %reshape.215, s32[16]{0:T(128)S(1)} %eq.152), kind=kOutput, calls=%fused_computation.7 | convolution fusion | flops 910712832 | bytes 37945408 | tf_op jit(solution)/shard_map/dot_general | solution.py:69
  54.8 18.7 %copy.33 = f32[3072,1536]{0,1:T(8,128)} copy(f32[3072,1536]{1,0:T(8,128)} %convolution_add_fusion) | data formatting | bytes 37748736 | tf_op jit(solution)/shard_map/add | solution.py:69
  73.4 8.2 gather_fusion.1
  81.9 6.3 stack.2
  88.3 5.5 all-to-all-start.2
  94.7 270.3 %all-to-all-done.2 = f32[8,3072,128]{1,2,0:T(8,128)} async-done(((f32[8,3072,128]{1,2,0:T(8,128)}), f32[8,3072,128]{1,2,0:T(8,128)}, u32[]{:S(2)}, u32[]{:S(2)}) %all-to-all-start.2) | async-done | bytes 12582944 | tf_op jit(solution)/shard_map/all_to_all | solution.py:87
  365.0 16.5 %gather_fusion.2 = f32[1024,3072]{1,0:T(8,128)} fusion(f32[3072,1024]{0,1:T(8,128)} %bitcast.10, s32[1024]{0:T(1024)S(1)} %broadcast_clamp_fusion), kind=kCustom, calls=%fused_computation.5 | custom fusion | bytes 25169920 | tf_op jit(solution)/shard_map/jit(_take)/gather | solution.py:90
  381.5 12.6 %copy.34 = f32[1024,3072]{0,1:T(8,128)} copy(f32[1024,3072]{1,0:T(8,128)} %gather_fusion.2) | data formatting | bytes 25165824 | tf_op jit(solution)/shard_map/jit(_take)/gather | solution.py:90
  394.1 12.4 %select_bitcast_fusion = f32[3072,1024]{1,0:T(8,128)} fusion(f32[1024,3072]{0,1:T(8,128)} %copy.34, pred[1024]{0:T(1024)(128)(4,1)S(1)} %compare_and_fusion.2), kind=kLoop, calls=%fused_computation.9 | loop fusion | flops 3145728 | bytes 25166848 | tf_op jit(solution)/shard_map/jit(_take)/select_n | solution.py:90
  406.5 4.8 fusion
  411.4 3.7 fusion.40
  415.1 2.3 copy.35
  417.4 5.3 gather_fusion.3
  424.3 5.2 multiply_add_fusion.3
  431.2 28.4 %all-reduce.14.cloned.1.call-done = f32[1024,256]{1,0:T(8,128)} async-done(((f32[1024,256]{1,0:T(8,128)}), f32[1024,256]{1,0:T(8,128)}) %all-reduce.14.cloned.1.call-update) | async-done | bytes 1048592 | tf_op jit(solution)/shard_map/psum | solution.py:120
  459.6 7.3 convolution_subtract_fusion.5
  467.0 4.1 fusion.13
  472.7 3.3 fusion.39
  476.0 3.5 copy.36
  479.6 6.5 gather_fusion.4
  486.1 2.5 select_select_fusion.1
  488.9 6.9 multiply_add_fusion.2
  495.9 8.0 convolution_subtract_fusion.4
  505.5 8.2 convolution_subtract_fusion.2
  513.8 11.8 %all-reduce.16.cloned.1.call-done = f32[1024,256]{1,0:T(8,128)} async-done(((f32[1024,256]{1,0:T(8,128)}), f32[1024,256]{1,0:T(8,128)}) %all-reduce.16.cloned.1.call-update) | async-done | bytes 1048592 | tf_op jit(solution)/shard_map/psum | solution.py:120
  525.6 8.3 %convolution_subtract_fusion.3 = f32[3072,256]{1,0:T(8,128)S(1)} fusion(f32[3072,256]{1,0:T(8,128)} %convolution_subtract_fusion.4, f32[3072,256]{0,1:T(8,128)} %multiply_add_fusion.2, f32[1024,256]{1,0:T(8,128)} %all-reduce.16.cloned.1.call-done), kind=kOutput, calls=%fused_computation.15 | convolution fusion | flops 2416705536 | bytes 9699328 | tf_op jit(solution)/shard_map/dot_general | solution.py:96
  533.9 4.1 fusion.11
  539.7 3.3 fusion.38
  543.0 3.5 copy.37
  546.5 6.5 gather_fusion.5
  553.0 2.6 select_select_fusion
  555.9 7.0 multiply_add_fusion.1
  565.4 8.1 convolution_subtract_fusion.1
  573.5 19.0 %all-reduce.18.cloned.1.call-done = f32[1024,256]{1,0:T(8,128)} async-done(((f32[1024,256]{1,0:T(8,128)}), f32[1024,256]{1,0:T(8,128)}) %all-reduce.18.cloned.1.call-update) | async-done | bytes 1048592 | tf_op jit(solution)/shard_map/psum | solution.py:120
  592.5 8.3 %convolution_subtract_fusion = f32[3072,256]{1,0:T(8,128)S(1)} fusion(f32[3072,256]{1,0:T(8,128)} %convolution_subtract_fusion.1, f32[3072,256]{0,1:T(8,128)} %multiply_add_fusion.1, f32[1024,256]{1,0:T(8,128)} %all-reduce.18.cloned.1.call-done), kind=kOutput, calls=%fused_computation.12 | convolution fusion | flops 2416705536 | bytes 9699328 | tf_op jit(solution)/shard_map/dot_general | solution.py:96
  600.9 4.3 fusion.9
  611.6 3.9 fusion.37
  620.2 5.1 pad_maximum_fusion
  625.3 12.6 %copy.38 = f32[3072,1024]{1,0:T(8,128)} copy(f32[3072,1024]{0,1:T(8,128)} %pad_maximum_fusion) | data formatting | bytes 25165824
  637.9 90.9 %all-reduce.20.cloned.1.call-done = (f32[1536,256]{0,1:T(8,128)}, f32[1536,256]{0,1:T(8,128)}, f32[1536,256]{0,1:T(8,128)}, f32[1536,256]{0,1:T(8,128)}) async-done(((f32[1536,256]{0,1:T(8,128)}, f32[1536,256]{0,1:T(8,128)}, f32[1536,256]{0,1:T(8,128)}, f32[1536,256]{0,1:T(8,128)}), (f32[1536,256]{0,1:T(8,128)}, f32[1536,256]{0,1:T(8,128)}, f32[1536,256]{0,1:T(8,128)}, ...) | async-done | bytes 6291472 | tf_op jit(solution)/shard_map/psum | solution.py:12
  728.8 19.9 %fusion.44 = f32[3072,1536]{1,0:T(8,128)} fusion(f32[3072,256]{0,1:T(8,128)} %multiply_add_fusion.1, f32[1536,256]{0,1:T(8,128)} %get-tuple-element.11), kind=kOutput, calls=%fused_computation.119 | convolution fusion | flops 14495514624 | bytes 23592960 | tf_op jit(solution)/shard_map/dot_general | solution.py:114
  748.6 18.5 %fusion.43 = f32[3072,1536]{1,0:T(8,128)} fusion(f32[3072,256]{0,1:T(8,128)S(1)} %copy-done.10, f32[1536,256]{0,1:T(8,128)S(1)} %copy-done.18), kind=kOutput, calls=%fused_computation.118 | convolution fusion | flops 14495514624 | bytes 23592960 | tf_op jit(solution)/shard_map/dot_general | solution.py:114
  767.1 17.9 %fusion.42 = f32[3072,1536]{1,0:T(8,128)} fusion(f32[3072,256]{0,1:T(8,128)S(1)} %multiply_add_fusion.3, f32[1536,256]{0,1:T(8,128)S(1)} %copy-done.17), kind=kOutput, calls=%fused_computation.117 | convolution fusion | flops 14495514624 | bytes 23592960 | tf_op jit(solution)/shard_map/dot_general | solution.py:114
  785.1 38.0 %subtract_select_fusion = f32[3072,1536]{1,0:T(8,128)} fusion(f32[3072,1536]{1,0:T(8,128)} %fusion.44, f32[3072,1536]{1,0:T(8,128)} %fusion.43, f32[3072,1536]{1,0:T(8,128)} %convolution_add_fusion, f32[3072,1536]{1,0:T(8,128)} %fusion.42, f32[3072,256]{0,1:T(8,128)} %copy-done.15, f32[1536,256]{0,1:T(8,128)} %get-tuple-element.14, ...), kind=kOutput, calls=%fused_computation.6 | convolution fusion | flops 14523826176 | bytes 99095040 | tf_op jit(solution)/shard_map/dot_general | solution.py:114
  (102 shorter events, 30.9 us)
Async XLA Ops:
  7.2 9.3 %copy-start = (f32[8,3072]{1,0:T(8,128)S(1)}, f32[8,3072]{1,0:T(8,128)}, u32[]{:S(2)}) copy-start(f32[8,3072]{1,0:T(8,128)} %param.11) | copy-start | bytes 294916
  9.2 13.7 %all-to-all-start.1 = ((s32[8,1,2]{2,1,0:T(1,128)}), s32[8,1,2]{2,1,0:T(1,128)S(1)}, u32[]{:S(2)}, u32[]{:S(2)}) async-start(s32[8,1,2]{2,1,0:T(1,128)} %copy.32), calls=%async_computation.1 | async-start | bytes 8192 | tf_op jit(solution)/shard_map/all_to_all | solution.py:63
  22.9 13.8 %all-to-all-start = ((f32[8,2,3072]{2,1,0:T(2,128)}), f32[8,2,3072]{2,1,0:T(2,128)S(1)}, u32[]{:S(2)}, u32[]{:S(2)}) async-start(f32[8,2,3072]{2,1,0:T(2,128)} %copy.31), calls=%async_computation | async-start | bytes 393216 | tf_op jit(solution)/shard_map/all_to_all | solution.py:62
  88.3 6.1 copy-start.20
  88.3 6.1 copy-start.21
  88.3 6.3 copy-start.11
  88.3 6.3 copy-start.22
  88.3 276.7 %all-to-all-start.2 = ((f32[8,3072,128]{1,2,0:T(8,128)}), f32[8,3072,128]{1,2,0:T(8,128)}, u32[]{:S(2)}, u32[]{:S(2)}) async-start(f32[8,3072,128]{1,2,0:T(8,128)} %stack.2), calls=%async_computation.2 | async-start | bytes 25165824 | tf_op jit(solution)/shard_map/all_to_all | solution.py:87
  93.8 365.8 %all-reduce.14.cloned.1.call-start = ((), (), s32[]{:S(2)}) async-start(), calls=%async_computation.3 | async-start | bytes 2097152 | tf_op jit(solution)/shard_map/psum | solution.py:120
  411.4 3.7 copy-start.6
  424.1 101.5 %all-reduce.16.cloned.1.call-start = ((), (), s32[]{:S(2)}) async-start(), calls=%async_computation.4 | async-start | bytes 2097152 | tf_op jit(solution)/shard_map/psum | solution.py:120
  424.3 5.2 copy-start.7
  471.1 1.7 copy-start.4
  488.7 103.9 %all-reduce.18.cloned.1.call-start = ((), (), s32[]{:S(2)}) async-start(), calls=%async_computation.5 | async-start | bytes 2097152 | tf_op jit(solution)/shard_map/psum | solution.py:120
  488.9 7.0 copy-start.19
  495.9 8.0 copy-start.5
  538.0 1.7 copy-start.2
  555.6 173.1 %all-reduce.20.cloned.1.call-start = ((), (), s32[]{:S(2)}) async-start(), calls=%async_computation.6 | async-start | bytes 12582912 | tf_op jit(solution)/shard_map/psum | solution.py:12
  555.9 7.1 copy-start.3
  555.9 8.7 %copy-start.16 = (f32[3072,256]{1,0:T(8,128)S(1)}, f32[3072,256]{1,0:T(8,128)}, u32[]{:S(2)}) copy-start(f32[3072,256]{1,0:T(8,128)} %convolution_subtract_fusion.2) | copy-start | bytes 9437188
  562.9 2.5 copy-start.8
  605.2 1.7 copy-start.12
  611.6 4.6 copy-start.13
  616.2 3.0 copy-start.9
  616.2 4.0 copy-start.14
  617.5 1.7 copy-start.15
  728.8 19.9 %copy-start.10 = (f32[3072,256]{0,1:T(8,128)S(1)}, f32[3072,256]{0,1:T(8,128)}, u32[]{:S(2)}) copy-start(f32[3072,256]{0,1:T(8,128)} %multiply_add_fusion.2) | copy-start | bytes 9437188
  728.8 19.9 %copy-start.18 = (f32[1536,256]{0,1:T(8,128)S(1)}, f32[1536,256]{0,1:T(8,128)}, u32[]{:S(2)}) copy-start(f32[1536,256]{0,1:T(8,128)} %get-tuple-element.12) | copy-start | bytes 4718596
  748.6 18.5 %copy-start.17 = (f32[1536,256]{0,1:T(8,128)S(1)}, f32[1536,256]{0,1:T(8,128)}, u32[]{:S(2)}) copy-start(f32[1536,256]{0,1:T(8,128)} %get-tuple-element.13) | copy-start | bytes 4718596
  785.1 38.1 %copy-start.1 = (f32[8,3072]{1,0:T(8,128)S(1)}, f32[8,3072]{1,0:T(8,128)}, u32[]{:S(2)}) copy-start(f32[8,3072]{1,0:T(8,128)} %param.11) | copy-start | bytes 294916
Sparse Core Ops, SparseCore 0:
  424.2 35.3 all-reduce.13
  488.8 36.7 all-reduce.15
  555.8 36.7 all-reduce.17
  608.6 120.0 all-reduce.19
